TPU v7x, 32 devices: a whole 2x2x4 slice. The times are simulated.
32 devices in a mesh: groups: 2 (over y), section: 4 (over z), replica: 4 (over x, core).
Axes of the slice: x: 2, y: 2, z: 4, core: 2. Of those that a mesh axis runs over, the one named last changes fastest.
Arguments:
- section_inputs: bfloat16 [8, 4, 2, 16, 16, 256], P(('groups', 'replica'), 'section'), parts along dimension 0, may hold values from -6 to 6
- cotangent: bfloat16 [8, 2, 16, 16, 256], P(('groups', 'replica')), parts along dimension 0, may hold values from -6 to 6
- crop_rows: int32 [8, 2], P(('groups', 'replica')), parts along dimension 0, may hold values from 0 to 705
- drift: bfloat16 [8, 4, 9, 256, 256], P(('groups', 'replica'), 'section'), parts along dimension 0, may hold values from -6 to 6
- params: float32 [8, 9, 256, 256], P(('groups', 'section')), parts along dimension 0, may hold values from -6 to 6
- momentum: float32 [8, 9, 256, 256], P(('groups', 'section'), None, 'replica'), parts along dimension 0, may hold values from -4 to 4
Outputs:
- new_params: float32 [8, 9, 256, 256], P(('groups', 'section')), parts along dimension 0
- new_momentum: float32 [8, 9, 256, 256], P(('groups', 'section'), None, 'replica'), parts along dimension 0
There are 2 independent parts, one for each index of `groups`. A program takes and returns all parts, laid end to end along the dimension named above; each array names one. Nothing has to cross between parts.
All inputs are finite; a program needn't handle non-finite values.
Results may differ from a plain program's by a relative error of at most 0.0075.
Values may be sent and summed in bfloat16 or wider, within the bound.
No kernel may reach another device: no remote copies, remote signals or barrier semaphores. Data moves between devices by JAX's collectives and lax.ppermute only.
A program may use at most 64 MiB of HBM per device.

v0:
```python
import math
import jax
import jax.numpy as jnp
from jax import lax
from jax.sharding import PartitionSpec as P

LATS = 721


def from_behind(x, axis, by):
    devices = lax.axis_size(axis)
    pairs = [(i, i + by) for i in range(devices) if 0 <= i + by < devices]
    return lax.ppermute(x, axis, pairs)


def lat_weight(first_row, count):
    rows = jnp.arange(count, dtype=jnp.float32) + first_row.astype(jnp.float32)
    middle = (LATS - 1) / 2.0
    every = jnp.arange(LATS, dtype=jnp.float32)
    norm_value = jnp.mean(jnp.cos(math.pi * (every - middle) / (LATS - 1)))
    return jnp.cos(math.pi * (rows - middle) / (LATS - 1)) / norm_value


def backward(inputs, out_grad, weights):
    rows, cols, width = inputs.shape
    scale = (9.0 * width) ** (-0.5)
    padded = jnp.pad(inputs, ((1, 1), (1, 1), (0, 0)))
    taps = jnp.stack([padded[a : a + rows, b : b + cols] for a in range(3) for b in range(3)])
    pre = jnp.einsum("krcd,kde->rce", taps, weights, preferred_element_type=jnp.float32) * scale
    tangent = jnp.tanh(pre)
    local = (out_grad.astype(jnp.float32) * (1.0 - tangent * tangent)).astype(jnp.bfloat16)
    grad = jnp.einsum("krcd,rce->kde", taps, local, preferred_element_type=jnp.float32) * scale
    back = jnp.einsum("rce,kde->krcd", local, weights, preferred_element_type=jnp.float32)
    accum = jnp.zeros((rows + 2, cols + 2, width), jnp.float32)
    for a in range(3):
        for b in range(3):
            accum = accum.at[a : a + rows, b : b + cols].add(back[3 * a + b])
    in_grad = (out_grad.astype(jnp.float32) + scale * accum[1 : rows + 1, 1 : cols + 1]).astype(
        jnp.bfloat16
    )
    return (grad, in_grad)


def per_device(section_inputs, cotangent, crop_rows, drift, params, momentum):
    section = lax.axis_index("section")
    sections = lax.axis_size("section")
    inputs_here = section_inputs[0, 0]
    cot_here = cotangent[0]
    crops_here = crop_rows[0]
    micro = inputs_here.shape[0]
    rows, cols, width = inputs_here.shape[1:]
    weights_bf = params[0].astype(jnp.bfloat16)

    def tick(step, carry):
        incoming, grad_total = carry
        micro_index = step - (sections - 1 - section)
        valid = jnp.logical_and(micro_index >= 0, micro_index < micro)
        chosen = jnp.clip(micro_index, 0, micro - 1)
        inputs_now = lax.dynamic_index_in_dim(inputs_here, chosen, 0, keepdims=False)
        cot_now = lax.dynamic_index_in_dim(cot_here, chosen, 0, keepdims=False)
        first_row = lax.dynamic_index_in_dim(crops_here, chosen, 0, keepdims=False)
        top_grad = (
            cot_now.astype(jnp.float32) * lat_weight(first_row, rows)[:, None, None]
        ).astype(jnp.bfloat16)
        out_grad = jnp.where(section == sections - 1, top_grad, incoming)
        contrib, in_grad = backward(inputs_now, out_grad, weights_bf)
        grad_total = grad_total + jnp.where(valid, contrib, jnp.zeros_like(contrib))
        passed = from_behind(in_grad, "section", -1)
        return (passed, grad_total)

    start = (
        jnp.zeros((rows, cols, width), jnp.bfloat16),
        jnp.zeros((9, width, width), jnp.float32),
    )
    unused, grad_total = lax.fori_loop(0, sections + micro - 1, tick, start)
    delta_bf = (drift[0, 0].astype(jnp.float32) + 0.5 * grad_total).astype(jnp.bfloat16)
    delta_bf = lax.optimization_barrier(delta_bf)
    delta = delta_bf.astype(jnp.float32)
    replicas = lax.axis_size("replica")
    here = lax.axis_index("replica")
    share_rows = width // replicas
    mean_delta = lax.psum(delta.astype(jnp.bfloat16), "replica").astype(jnp.float32) / replicas
    mom_whole = lax.all_gather(momentum[0], "replica", axis=1, tiled=True)
    mom_next = 0.9 * mom_whole + mean_delta
    new_params = params[0] - 0.7 * (mean_delta + 0.9 * mom_next)
    new_momentum = lax.dynamic_slice_in_dim(mom_next, here * share_rows, share_rows, 1)
    return (new_params[None], new_momentum[None])


def solution(mesh):
    placed = (
        P(("groups", "replica"), "section", None, None, None, None),
        P(("groups", "replica"), None, None, None, None),
        P(("groups", "replica"), None),
        P(("groups", "replica"), "section", None, None, None),
        P(("groups", "section"), None, None, None),
        P(("groups", "section"), None, "replica", None),
    )
    return jax.shard_map(
        per_device,
        mesh=mesh,
        in_specs=placed,
        out_specs=(
            P(("groups", "section"), None, None, None),
            P(("groups", "section"), None, "replica", None),
        ),
        check_vma=False,
    )
```

profile of v0, /device:TPU:0, one launch (start us, length us, event | category | flops | bytes accessed | tf_op | source)
XLA Modules:
  0.0 208.0 jit_solution(15496415123760340458)
XLA Ops:
  7.3 1.8 bitcast_convert_fusion
  9.1 119.2 %while.28 = (s32[]{:T(128)}, bf16[16,16,256]{2,1,0:T(8,128)(2,1)S(1)}, f32[9,256,256]{2,1,0:T(8,128)}, pred[]{:T(512)}, s32[]{:T(128)}, /*index=5*/bf16[2,16,16,...) while((s32[]{:T(128)}, ...), condition=%wide.region_3.4_spmd.clone, body=%wide.region_0.3_spmd.clone.sunk | while | flops 910100672 | bytes 44110644 | solution.py:75
  9.2 0.9 cosine_reduce_fusion.2
  12.6 1.4 fusion.102
  15.9 1.3 fusion.104
  17.2 1.6 scatter-add.71
  18.8 0.8 and_reduce_fusion.2
  19.5 1.9 add_select_fusion.2
  21.4 1.6 scatter-add.72
  24.8 1.1 fusion.112
  25.8 1.3 collective-permute-start
  27.2 3.4 %fusion.113 = f32[9,256,256]{2,1,0:T(8,128)} fusion(f32[9,256,256]{2,1,0:T(8,128)} %get-tuple-element.608, bf16[9,16,16,256]{3,2,0,1:T(8,128)(2,1)} %copy-done.7, pred[]{:T(512)S(6)} %compare.180, pred[]{:T(512)S(6)} %and.113, bf16[16,16,256]{2,1,0:T(8,128)(2,1)} %copy-done.6), kind=kOutput, calls=%fused_computation.2.clone.1 | convolution fusion | flops 304349184 | bytes 6029314 | tf_op jit(solution)/shard_map/while/body/eval_jaxpr/krcd,rce->kde/dot_general | solution.py:32
  30.6 3.7 %collective-permute-done = bf16[16,16,256]{2,1,0:T(8,128)(2,1)S(1)} collective-permute-done((bf16[16,16,256]{2,1,0:T(8,128)(2,1)S(1)}, bf16[16,16,256]{2,1,0:T(8,128)(2,1)S(1)}, u32[]{:S(2)}, u32[]{:S(2)}) %collective-permute-start) | collective-permute-done | bytes 131104 | tf_op jit(solution)/shard_map/while/body/eval_jaxpr/ppermute | solution.py:13
  34.3 0.9 cosine_reduce_fusion.2
  35.5 0.7 dynamic_slice.59
  37.7 1.4 fusion.102
  41.0 1.3 fusion.104
  42.3 1.6 scatter-add.71
  43.9 0.8 and_reduce_fusion.2
  44.6 1.9 add_select_fusion.2
  46.5 1.6 scatter-add.72
  49.8 1.1 fusion.112
  50.9 1.3 collective-permute-start
  52.3 4.2 %fusion.113 = f32[9,256,256]{2,1,0:T(8,128)} fusion(f32[9,256,256]{2,1,0:T(8,128)} %get-tuple-element.608, bf16[9,16,16,256]{3,2,0,1:T(8,128)(2,1)} %copy-done.7, pred[]{:T(512)S(6)} %compare.180, pred[]{:T(512)S(6)} %and.113, bf16[16,16,256]{2,1,0:T(8,128)(2,1)} %copy-done.6), kind=kOutput, calls=%fused_computation.2.clone.1 | convolution fusion | flops 304349184 | bytes 6029314 | tf_op jit(solution)/shard_map/while/body/eval_jaxpr/krcd,rce->kde/dot_general | solution.py:32
  56.5 1.3 collective-permute-done
  57.8 0.9 cosine_reduce_fusion.2
  61.2 1.4 fusion.102
  64.5 1.3 fusion.104
  65.8 1.6 scatter-add.71
  67.4 0.8 and_reduce_fusion.2
  68.2 1.9 add_select_fusion.2
  70.1 1.6 scatter-add.72
  73.4 1.1 fusion.112
  74.5 1.3 collective-permute-start
  75.8 4.2 %fusion.113 = f32[9,256,256]{2,1,0:T(8,128)} fusion(f32[9,256,256]{2,1,0:T(8,128)} %get-tuple-element.608, bf16[9,16,16,256]{3,2,0,1:T(8,128)(2,1)} %copy-done.7, pred[]{:T(512)S(6)} %compare.180, pred[]{:T(512)S(6)} %and.113, bf16[16,16,256]{2,1,0:T(8,128)(2,1)} %copy-done.6), kind=kOutput, calls=%fused_computation.2.clone.1 | convolution fusion | flops 304349184 | bytes 6029314 | tf_op jit(solution)/shard_map/while/body/eval_jaxpr/krcd,rce->kde/dot_general | solution.py:32
  80.0 1.3 collective-permute-done
  81.3 0.9 cosine_reduce_fusion.2
  82.6 0.7 dynamic_slice.59
  84.7 1.4 fusion.102
  88.0 1.3 fusion.104
  89.3 1.6 scatter-add.71
  90.9 0.8 and_reduce_fusion.2
  91.7 1.9 add_select_fusion.2
  93.6 1.6 scatter-add.72
  96.9 1.1 fusion.112
  98.0 1.3 collective-permute-start
  99.3 4.2 %fusion.113 = f32[9,256,256]{2,1,0:T(8,128)} fusion(f32[9,256,256]{2,1,0:T(8,128)} %get-tuple-element.608, bf16[9,16,16,256]{3,2,0,1:T(8,128)(2,1)} %copy-done.7, pred[]{:T(512)S(6)} %compare.180, pred[]{:T(512)S(6)} %and.113, bf16[16,16,256]{2,1,0:T(8,128)(2,1)} %copy-done.6), kind=kOutput, calls=%fused_computation.2.clone.1 | convolution fusion | flops 304349184 | bytes 6029314 | tf_op jit(solution)/shard_map/while/body/eval_jaxpr/krcd,rce->kde/dot_general | solution.py:32
  103.5 1.3 collective-permute-done
  104.9 0.9 cosine_reduce_fusion.2
  108.2 1.4 fusion.102
  111.6 1.3 fusion.104
  112.9 1.6 scatter-add.71
  114.5 0.8 and_reduce_fusion.2
  115.2 1.9 add_select_fusion.2
  117.1 1.6 scatter-add.72
  120.4 1.1 fusion.112
  121.5 1.3 collective-permute-start
  122.9 4.2 %fusion.113 = f32[9,256,256]{2,1,0:T(8,128)} fusion(f32[9,256,256]{2,1,0:T(8,128)} %get-tuple-element.608, bf16[9,16,16,256]{3,2,0,1:T(8,128)(2,1)} %copy-done.7, pred[]{:T(512)S(6)} %compare.180, pred[]{:T(512)S(6)} %and.113, bf16[16,16,256]{2,1,0:T(8,128)(2,1)} %copy-done.6), kind=kOutput, calls=%fused_computation.2.clone.1 | convolution fusion | flops 304349184 | bytes 6029314 | tf_op jit(solution)/shard_map/while/body/eval_jaxpr/krcd,rce->kde/dot_general | solution.py:32
  127.1 1.3 collective-permute-done
  128.4 3.5 %fusion.56 = bf16[9,256,256]{2,1,0:T(8,128)(2,1)} fusion(f32[9,256,256]{2,1,0:T(8,128)} %get-tuple-element.472, bf16[1,1,9,256,256]{4,3,2,1,0:T(8,128)(2,1)} %param.29), kind=kLoop, calls=%fused_computation.72 | loop fusion | flops 2359296 | bytes 4718592 | tf_op jit(solution)/shard_map/convert_element_type | solution.py:76
  132.6 37.8 %all-reduce.4.cloned.1.call-done = bf16[9,256,256]{2,1,0:T(8,128)(2,1)} async-done(((bf16[9,256,256]{2,1,0:T(8,128)(2,1)}), bf16[9,256,256]{2,1,0:T(8,128)(2,1)}) %all-reduce.4.cloned.1.call-update) | async-done | bytes 1179664 | tf_op jit(solution)/shard_map/psum | solution.py:82
  170.5 25.8 %all-gather.3.cloned.1.call-done = f32[1,9,256,256]{3,2,1,0:T(8,128)} async-done(((f32[1,9,64,256]{3,2,1,0:T(8,128)}), f32[1,9,256,256]{3,2,1,0:T(8,128)}) %all-gather.3.cloned.1.call-update) | async-done | bytes 2359312 | tf_op jit(solution)/shard_map/all_gather | solution.py:83
  196.3 4.0 %bitcast_add_fusion = (f32[9,256,256]{2,1,0:T(8,128)S(1)}, f32[1,9,256,256]{3,2,1,0:T(8,128)}) fusion(f32[1,9,256,256]{3,2,1,0:T(8,128)} %all-gather.3.cloned.1.call-done, bf16[9,256,256]{2,1,0:T(8,128)(2,1)} %all-reduce.4.cloned.1.call-done, f32[1,9,256,256]{3,2,1,0:T(8,128)S(1)} %copy-done.4), kind=kLoop, calls=%fused_computation.73 | loop fusion | flops 4718592 | bytes 10616832 | tf_op jit(solution)/shard_map/add | solution.py:84
  200.3 0.9 dynamic-slice_bitcast_fusion.1
  (228 shorter events, 22.2 us)
Async XLA Ops:
  7.2 2.0 copy-start.9
  7.2 1.9 copy-start.8
  7.2 2.0 copy-start.10
  7.2 163.3 %all-reduce.4.cloned.1.call-start = ((), (), s32[]{:S(2)}) async-start(), calls=%async_computation | async-start | bytes 2359296 | tf_op jit(solution)/shard_map/psum | solution.py:82
  9.2 3.4 %copy-start.2 = (bf16[2,16,16,256]{3,2,0,1:T(8,128)(2,1)}, bf16[2,16,16,256]{3,2,0,1:T(8,128)(2,1)S(1)}, u32[]{:S(2)}) copy-start(bf16[2,16,16,256]{3,2,0,1:T(8,128)(2,1)S(1)} %get-tuple-element.629) | copy-start | bytes 786436 | tf_op jit(solution)/shard_map/while
  9.2 3.4 %copy-start.5 = (bf16[16,16,256]{2,1,0:T(8,128)(2,1)}, bf16[16,16,256]{2,1,0:T(8,128)(2,1)S(1)}, u32[]{:S(2)}) copy-start(bf16[16,16,256]{2,1,0:T(8,128)(2,1)S(1)} %get-tuple-element.607) | copy-start | bytes 393220 | tf_op jit(solution)/shard_map/while
  9.2 4.8 %copy-start = (bf16[9,256,256]{2,1,0:T(8,128)(2,1)}, bf16[9,256,256]{2,1,0:T(8,128)(2,1)S(1)}, u32[]{:S(2)}) copy-start(bf16[9,256,256]{2,1,0:T(8,128)(2,1)S(1)} %get-tuple-element.630) | copy-start | bytes 3538948 | tf_op jit(solution)/shard_map/while
  10.4 2.1 %copy-start.7 = (bf16[9,16,16,256]{3,2,0,1:T(8,128)(2,1)}, bf16[9,16,16,256]{3,2,0,1:T(8,128)(2,1)S(1)}, u32[]{:S(2)}) copy-start(bf16[9,16,16,256]{3,2,0,1:T(8,128)(2,1)S(1)} %fusion.101) | copy-start | bytes 3538948 | tf_op jit(solution)/shard_map/while
  14.0 1.9 copy-start.6
  25.8 8.4 %collective-permute-start = (bf16[16,16,256]{2,1,0:T(8,128)(2,1)S(1)}, bf16[16,16,256]{2,1,0:T(8,128)(2,1)S(1)}, u32[]{:S(2)}, u32[]{:S(2)}) collective-permute-start(bf16[16,16,256]{2,1,0:T(8,128)(2,1)S(1)} %fusion.112), channel_id=1, source_target_pairs={{4,0},{8,4},{12,8},{5,1},{9,5},{13,9},{6,2},{10,6},{14,10},{7,3},{... | collective-permute-start | bytes 393224 | tf_op jit(solution)/shard_map/while/body/eval_jaxpr/ppermute | solution.py:13
  27.2 7.1 %copy-start.1 = (bf16[9,256,256]{2,1,0:T(8,128)(2,1)S(1)}, bf16[9,256,256]{2,1,0:T(8,128)(2,1)}, u32[]{:S(2)}) copy-start(bf16[9,256,256]{2,1,0:T(8,128)(2,1)} %copy-done) | copy-start | bytes 3538948 | tf_op jit(solution)/shard_map/while
  27.2 7.1 %copy-start.3 = (bf16[2,16,16,256]{3,2,0,1:T(8,128)(2,1)S(1)}, bf16[2,16,16,256]{3,2,0,1:T(8,128)(2,1)}, u32[]{:S(2)}) copy-start(bf16[2,16,16,256]{3,2,0,1:T(8,128)(2,1)} %copy-done.2) | copy-start | bytes 786436 | tf_op jit(solution)/shard_map/while
  34.3 3.4 %copy-start.2 = (bf16[2,16,16,256]{3,2,0,1:T(8,128)(2,1)}, bf16[2,16,16,256]{3,2,0,1:T(8,128)(2,1)S(1)}, u32[]{:S(2)}) copy-start(bf16[2,16,16,256]{3,2,0,1:T(8,128)(2,1)S(1)} %get-tuple-element.629) | copy-start | bytes 786436 | tf_op jit(solution)/shard_map/while
  34.3 3.4 %copy-start.5 = (bf16[16,16,256]{2,1,0:T(8,128)(2,1)}, bf16[16,16,256]{2,1,0:T(8,128)(2,1)S(1)}, u32[]{:S(2)}) copy-start(bf16[16,16,256]{2,1,0:T(8,128)(2,1)S(1)} %get-tuple-element.607) | copy-start | bytes 393220 | tf_op jit(solution)/shard_map/while
  34.3 4.8 %copy-start = (bf16[9,256,256]{2,1,0:T(8,128)(2,1)}, bf16[9,256,256]{2,1,0:T(8,128)(2,1)S(1)}, u32[]{:S(2)}) copy-start(bf16[9,256,256]{2,1,0:T(8,128)(2,1)S(1)} %get-tuple-element.630) | copy-start | bytes 3538948 | tf_op jit(solution)/shard_map/while
  35.5 2.1 %copy-start.7 = (bf16[9,16,16,256]{3,2,0,1:T(8,128)(2,1)}, bf16[9,16,16,256]{3,2,0,1:T(8,128)(2,1)S(1)}, u32[]{:S(2)}) copy-start(bf16[9,16,16,256]{3,2,0,1:T(8,128)(2,1)S(1)} %fusion.101) | copy-start | bytes 3538948 | tf_op jit(solution)/shard_map/while
  39.1 1.9 copy-start.6
  50.9 6.9 %collective-permute-start = (bf16[16,16,256]{2,1,0:T(8,128)(2,1)S(1)}, bf16[16,16,256]{2,1,0:T(8,128)(2,1)S(1)}, u32[]{:S(2)}, u32[]{:S(2)}) collective-permute-start(bf16[16,16,256]{2,1,0:T(8,128)(2,1)S(1)} %fusion.112), channel_id=1, source_target_pairs={{4,0},{8,4},{12,8},{5,1},{9,5},{13,9},{6,2},{10,6},{14,10},{7,3},{... | collective-permute-start | bytes 393224 | tf_op jit(solution)/shard_map/while/body/eval_jaxpr/ppermute | solution.py:13
  52.2 5.6 %copy-start.1 = (bf16[9,256,256]{2,1,0:T(8,128)(2,1)S(1)}, bf16[9,256,256]{2,1,0:T(8,128)(2,1)}, u32[]{:S(2)}) copy-start(bf16[9,256,256]{2,1,0:T(8,128)(2,1)} %copy-done) | copy-start | bytes 3538948 | tf_op jit(solution)/shard_map/while
  52.3 5.5 %copy-start.3 = (bf16[2,16,16,256]{3,2,0,1:T(8,128)(2,1)S(1)}, bf16[2,16,16,256]{3,2,0,1:T(8,128)(2,1)}, u32[]{:S(2)}) copy-start(bf16[2,16,16,256]{3,2,0,1:T(8,128)(2,1)} %copy-done.2) | copy-start | bytes 786436 | tf_op jit(solution)/shard_map/while
  57.8 3.4 %copy-start.2 = (bf16[2,16,16,256]{3,2,0,1:T(8,128)(2,1)}, bf16[2,16,16,256]{3,2,0,1:T(8,128)(2,1)S(1)}, u32[]{:S(2)}) copy-start(bf16[2,16,16,256]{3,2,0,1:T(8,128)(2,1)S(1)} %get-tuple-element.629) | copy-start | bytes 786436 | tf_op jit(solution)/shard_map/while
  57.8 3.4 %copy-start.5 = (bf16[16,16,256]{2,1,0:T(8,128)(2,1)}, bf16[16,16,256]{2,1,0:T(8,128)(2,1)S(1)}, u32[]{:S(2)}) copy-start(bf16[16,16,256]{2,1,0:T(8,128)(2,1)S(1)} %get-tuple-element.607) | copy-start | bytes 393220 | tf_op jit(solution)/shard_map/while
  57.8 4.8 %copy-start = (bf16[9,256,256]{2,1,0:T(8,128)(2,1)}, bf16[9,256,256]{2,1,0:T(8,128)(2,1)S(1)}, u32[]{:S(2)}) copy-start(bf16[9,256,256]{2,1,0:T(8,128)(2,1)S(1)} %get-tuple-element.630) | copy-start | bytes 3538948 | tf_op jit(solution)/shard_map/while
  59.0 2.1 %copy-start.7 = (bf16[9,16,16,256]{3,2,0,1:T(8,128)(2,1)}, bf16[9,16,16,256]{3,2,0,1:T(8,128)(2,1)S(1)}, u32[]{:S(2)}) copy-start(bf16[9,16,16,256]{3,2,0,1:T(8,128)(2,1)S(1)} %fusion.101) | copy-start | bytes 3538948 | tf_op jit(solution)/shard_map/while
  62.6 1.9 copy-start.6
  74.5 6.9 %collective-permute-start = (bf16[16,16,256]{2,1,0:T(8,128)(2,1)S(1)}, bf16[16,16,256]{2,1,0:T(8,128)(2,1)S(1)}, u32[]{:S(2)}, u32[]{:S(2)}) collective-permute-start(bf16[16,16,256]{2,1,0:T(8,128)(2,1)S(1)} %fusion.112), channel_id=1, source_target_pairs={{4,0},{8,4},{12,8},{5,1},{9,5},{13,9},{6,2},{10,6},{14,10},{7,3},{... | collective-permute-start | bytes 393224 | tf_op jit(solution)/shard_map/while/body/eval_jaxpr/ppermute | solution.py:13
  75.8 5.6 %copy-start.1 = (bf16[9,256,256]{2,1,0:T(8,128)(2,1)S(1)}, bf16[9,256,256]{2,1,0:T(8,128)(2,1)}, u32[]{:S(2)}) copy-start(bf16[9,256,256]{2,1,0:T(8,128)(2,1)} %copy-done) | copy-start | bytes 3538948 | tf_op jit(solution)/shard_map/while
  75.8 5.5 %copy-start.3 = (bf16[2,16,16,256]{3,2,0,1:T(8,128)(2,1)S(1)}, bf16[2,16,16,256]{3,2,0,1:T(8,128)(2,1)}, u32[]{:S(2)}) copy-start(bf16[2,16,16,256]{3,2,0,1:T(8,128)(2,1)} %copy-done.2) | copy-start | bytes 786436 | tf_op jit(solution)/shard_map/while
  81.3 3.4 %copy-start.2 = (bf16[2,16,16,256]{3,2,0,1:T(8,128)(2,1)}, bf16[2,16,16,256]{3,2,0,1:T(8,128)(2,1)S(1)}, u32[]{:S(2)}) copy-start(bf16[2,16,16,256]{3,2,0,1:T(8,128)(2,1)S(1)} %get-tuple-element.629) | copy-start | bytes 786436 | tf_op jit(solution)/shard_map/while
  81.3 3.4 %copy-start.5 = (bf16[16,16,256]{2,1,0:T(8,128)(2,1)}, bf16[16,16,256]{2,1,0:T(8,128)(2,1)S(1)}, u32[]{:S(2)}) copy-start(bf16[16,16,256]{2,1,0:T(8,128)(2,1)S(1)} %get-tuple-element.607) | copy-start | bytes 393220 | tf_op jit(solution)/shard_map/while
  81.3 4.8 %copy-start = (bf16[9,256,256]{2,1,0:T(8,128)(2,1)}, bf16[9,256,256]{2,1,0:T(8,128)(2,1)S(1)}, u32[]{:S(2)}) copy-start(bf16[9,256,256]{2,1,0:T(8,128)(2,1)S(1)} %get-tuple-element.630) | copy-start | bytes 3538948 | tf_op jit(solution)/shard_map/while
  82.6 2.1 %copy-start.7 = (bf16[9,16,16,256]{3,2,0,1:T(8,128)(2,1)}, bf16[9,16,16,256]{3,2,0,1:T(8,128)(2,1)S(1)}, u32[]{:S(2)}) copy-start(bf16[9,16,16,256]{3,2,0,1:T(8,128)(2,1)S(1)} %fusion.101) | copy-start | bytes 3538948 | tf_op jit(solution)/shard_map/while
  86.1 1.9 copy-start.6
  98.0 6.9 %collective-permute-start = (bf16[16,16,256]{2,1,0:T(8,128)(2,1)S(1)}, bf16[16,16,256]{2,1,0:T(8,128)(2,1)S(1)}, u32[]{:S(2)}, u32[]{:S(2)}) collective-permute-start(bf16[16,16,256]{2,1,0:T(8,128)(2,1)S(1)} %fusion.112), channel_id=1, source_target_pairs={{4,0},{8,4},{12,8},{5,1},{9,5},{13,9},{6,2},{10,6},{14,10},{7,3},{... | collective-permute-start | bytes 393224 | tf_op jit(solution)/shard_map/while/body/eval_jaxpr/ppermute | solution.py:13
  99.3 5.6 %copy-start.1 = (bf16[9,256,256]{2,1,0:T(8,128)(2,1)S(1)}, bf16[9,256,256]{2,1,0:T(8,128)(2,1)}, u32[]{:S(2)}) copy-start(bf16[9,256,256]{2,1,0:T(8,128)(2,1)} %copy-done) | copy-start | bytes 3538948 | tf_op jit(solution)/shard_map/while
  99.3 5.5 %copy-start.3 = (bf16[2,16,16,256]{3,2,0,1:T(8,128)(2,1)S(1)}, bf16[2,16,16,256]{3,2,0,1:T(8,128)(2,1)}, u32[]{:S(2)}) copy-start(bf16[2,16,16,256]{3,2,0,1:T(8,128)(2,1)} %copy-done.2) | copy-start | bytes 786436 | tf_op jit(solution)/shard_map/while
  104.9 3.4 %copy-start.2 = (bf16[2,16,16,256]{3,2,0,1:T(8,128)(2,1)}, bf16[2,16,16,256]{3,2,0,1:T(8,128)(2,1)S(1)}, u32[]{:S(2)}) copy-start(bf16[2,16,16,256]{3,2,0,1:T(8,128)(2,1)S(1)} %get-tuple-element.629) | copy-start | bytes 786436 | tf_op jit(solution)/shard_map/while
  104.9 3.4 %copy-start.5 = (bf16[16,16,256]{2,1,0:T(8,128)(2,1)}, bf16[16,16,256]{2,1,0:T(8,128)(2,1)S(1)}, u32[]{:S(2)}) copy-start(bf16[16,16,256]{2,1,0:T(8,128)(2,1)S(1)} %get-tuple-element.607) | copy-start | bytes 393220 | tf_op jit(solution)/shard_map/while
  104.9 4.8 %copy-start = (bf16[9,256,256]{2,1,0:T(8,128)(2,1)}, bf16[9,256,256]{2,1,0:T(8,128)(2,1)S(1)}, u32[]{:S(2)}) copy-start(bf16[9,256,256]{2,1,0:T(8,128)(2,1)S(1)} %get-tuple-element.630) | copy-start | bytes 3538948 | tf_op jit(solution)/shard_map/while
  106.1 2.1 %copy-start.7 = (bf16[9,16,16,256]{3,2,0,1:T(8,128)(2,1)}, bf16[9,16,16,256]{3,2,0,1:T(8,128)(2,1)S(1)}, u32[]{:S(2)}) copy-start(bf16[9,16,16,256]{3,2,0,1:T(8,128)(2,1)S(1)} %fusion.101) | copy-start | bytes 3538948 | tf_op jit(solution)/shard_map/while
  109.7 1.9 copy-start.6
  121.5 6.9 %collective-permute-start = (bf16[16,16,256]{2,1,0:T(8,128)(2,1)S(1)}, bf16[16,16,256]{2,1,0:T(8,128)(2,1)S(1)}, u32[]{:S(2)}, u32[]{:S(2)}) collective-permute-start(bf16[16,16,256]{2,1,0:T(8,128)(2,1)S(1)} %fusion.112), channel_id=1, source_target_pairs={{4,0},{8,4},{12,8},{5,1},{9,5},{13,9},{6,2},{10,6},{14,10},{7,3},{... | collective-permute-start | bytes 393224 | tf_op jit(solution)/shard_map/while/body/eval_jaxpr/ppermute | solution.py:13
  122.8 5.6 %copy-start.1 = (bf16[9,256,256]{2,1,0:T(8,128)(2,1)S(1)}, bf16[9,256,256]{2,1,0:T(8,128)(2,1)}, u32[]{:S(2)}) copy-start(bf16[9,256,256]{2,1,0:T(8,128)(2,1)} %copy-done) | copy-start | bytes 3538948 | tf_op jit(solution)/shard_map/while
  122.9 5.5 %copy-start.3 = (bf16[2,16,16,256]{3,2,0,1:T(8,128)(2,1)S(1)}, bf16[2,16,16,256]{3,2,0,1:T(8,128)(2,1)}, u32[]{:S(2)}) copy-start(bf16[2,16,16,256]{3,2,0,1:T(8,128)(2,1)} %copy-done.2) | copy-start | bytes 786436 | tf_op jit(solution)/shard_map/while
  128.4 67.9 %copy-start.4 = (f32[1,9,256,256]{3,2,1,0:T(8,128)S(1)}, f32[1,9,256,256]{3,2,1,0:T(8,128)}, u32[]{:S(2)}) copy-start(f32[1,9,256,256]{3,2,1,0:T(8,128)} %param.30) | copy-start | bytes 7077892
  131.9 64.4 %all-gather.3.cloned.1.call-start = ((), (), s32[]{:S(2)}) async-start(), calls=%async_computation.1 | async-start | bytes 2949120 | tf_op jit(solution)/shard_map/all_gather | solution.py:83
Sparse Core Ops, SparseCore 0:
  132.0 38.4 all-reduce.3
  172.0 24.1 all-gather.2
where the time goes:
time: 209 us; the launch traced here: 208 us
  waiting for transfers between devices  73.4 us (35%)
  other arithmetic  40.8 us (20%)
  local copies, waits for them, and re-layouts  35.3 us (17%)
  matrix products  29.7 us (14%)
  between operations  14.1 us (7%)
  loops' own time  8.19 us (4%)
  starting transfers between devices  6.54 us (3%)
    psum x1, waiting for transfers between devices, per_device(): lax.psum(delta.astype(jnp.bfloat16), 'replica').astype(jnp.float32)  37.8 us
    all_gather x1, waiting for transfers between devices, per_device(): mom_whole = lax.all_gather(momentum[0], 'replica', axis=1, tiled=True)  25.8 us
    scatter-add x35, local copies, waits for them, and re-layouts, backward(): accum = accum.at[a:a + rows, b:b + cols].add(back[3 * a + b])  22.7 us
    dot_general x5, matrix products, backward(): jnp.einsum('krcd,rce->kde', taps, local, preferred_element_type=jnp.float32)  20.2 us
    another operation x15, other arithmetic  13.3 us
    ppermute x5, waiting for transfers between devices, from_behind(): return lax.ppermute(x, axis, pairs)  9.02 us
    another operation x1, loops' own time, per_device(): unused, grad_total = lax.fori_loop(0, sections + micro - 1, tick, start)  8.19 us
    add x25, other arithmetic, backward(): accum = accum.at[a:a + rows, b:b + cols].add(back[3 * a + b])  7.39 us
  transfers between devices with their start and end apart: 7, of which 7 were waited for; matrix products, arithmetic and copies ran while one was open for 10% of the time, Pallas kernels for 0%

commit v1 on v0

--- a/solution.py
+++ b/solution.py
@@ -80,7 +80,24 @@
     here = lax.axis_index("replica")
     share_rows = width // replicas
     mean_delta = lax.psum(delta.astype(jnp.bfloat16), "replica").astype(jnp.float32) / replicas
-    mom_whole = lax.all_gather(momentum[0], "replica", axis=1, tiled=True)
+    ways, here_2, k = (lax.axis_size("replica"), lax.axis_index("replica"), momentum[0].shape[1])
+    shape = [n * ways if d == 1 else n for d, n in enumerate(momentum[0].shape)]
+    mom_whole = lax.dynamic_update_slice_in_dim(
+        jnp.zeros(shape, momentum[0].dtype), momentum[0], here_2 * k, axis=1
+    )
+    going_up = going_down = momentum[0]
+    for far in range(1, ways // 2 + 1):
+        going_up = lax.ppermute(going_up, "replica", [(d, (d + 1) % ways) for d in range(ways)])
+        mom_whole = lax.dynamic_update_slice_in_dim(
+            mom_whole, going_up, (here_2 - far) % ways * k, axis=1
+        )
+        if 2 * far < ways:
+            going_down = lax.ppermute(
+                going_down, "replica", [(d, (d - 1) % ways) for d in range(ways)]
+            )
+            mom_whole = lax.dynamic_update_slice_in_dim(
+                mom_whole, going_down, (here_2 + far) % ways * k, axis=1
+            )
     mom_next = 0.9 * mom_whole + mean_delta
     new_params = params[0] - 0.7 * (mean_delta + 0.9 * mom_next)
     new_momentum = lax.dynamic_slice_in_dim(mom_next, here * share_rows, share_rows, 1)

time: 209 us -> 196 us (0.938)
  waiting for transfers between devices: 73.4 us -> 46.4 us
  local copies, waits for them, and re-layouts: 35.3 us -> 44.7 us
  starting transfers between devices: 6.54 us -> 11.5 us
    all_gather x1 -> x0, waiting for transfers between devices: 25.8 us -> none  [per_device(): mom_whole = lax.all_gather(momentum[0], 'replica', axis=1, tiled=True)]
    psum x1, waiting for transfers between devices: 37.8 us -> 28.5 us  [per_device(): lax.psum(delta.astype(jnp.bfloat16), 'replica').astype(jnp.float32)]
    ppermute x0 -> x3, waiting for transfers between devices: none -> 8.71 us  [the longest x2 8.71 us: per_device(): lax.ppermute(going_up, 'replica', [(d, (d + 1) % ways) for d in range(way...]
    dynamic_update_slice x0 -> x4, local copies, waits for them, and re-layouts: none -> 6.7 us  [the longest x2 3.88 us: per_device(): lax.dynamic_update_slice_in_dim(mom_whole, going_up, (here_2 - far) % way...]
    ppermute x0 -> x3, starting transfers between devices: none -> 5.01 us  [the longest x2 3.01 us: per_device(): lax.ppermute(going_up, 'replica', [(d, (d + 1) % ways) for d in range(way...]
    another operation x15 -> x16, local copies, waits for them, and re-layouts: 6.44 us -> 8.13 us
  transfers between devices with their start and end apart: 7 -> 9, of which waited for: 7 -> 7; matrix products, arithmetic and copies ran while one was open for 10% -> 56% of each run, Pallas kernels for 0% -> 0%
where the time goes in v1:
time: 196 us; the launch traced here: 195 us
  waiting for transfers between devices  46.4 us (24%)
  local copies, waits for them, and re-layouts  44.7 us (23%)
  other arithmetic  40.6 us (21%)
  matrix products  29.7 us (15%)
  between operations  14.1 us (7%)
  starting transfers between devices  11.5 us (6%)
  loops' own time  7.98 us (4%)
    psum x1, waiting for transfers between devices, per_device(): lax.psum(delta.astype(jnp.bfloat16), 'replica').astype(jnp.float32)  28.5 us
    scatter-add x35, local copies, waits for them, and re-layouts, backward(): accum = accum.at[a:a + rows, b:b + cols].add(back[3 * a + b])  22.8 us
    dot_general x5, matrix products, backward(): jnp.einsum('krcd,rce->kde', taps, local, preferred_element_type=jnp.float32)  20.2 us
    another operation x15, other arithmetic  13.9 us
    ppermute x5, waiting for transfers between devices, from_behind(): return lax.ppermute(x, axis, pairs)  9.15 us
    ppermute x2, waiting for transfers between devices, per_device(): lax.ppermute(going_up, 'replica', [(d, (d + 1) % ways) for d in range(way...  8.71 us
    another operation x16, local copies, waits for them, and re-layouts  8.13 us
    another operation x1, loops' own time, per_device(): unused, grad_total = lax.fori_loop(0, sections + micro - 1, tick, start)  7.98 us
  transfers between devices with their start and end apart: 9, of which 7 were waited for; matrix products, arithmetic and copies ran while one was open for 56% of the time, Pallas kernels for 0%

profile of v1, /device:TPU:0, one launch (start us, length us, event | category | flops | bytes accessed | tf_op | source)
XLA Modules:
  0.0 195.0 jit_solution(11019723705923721432)
XLA Ops:
  7.7 2.0 %collective-permute-start.2 = (f32[9,64,256]{2,1,0:T(8,128)}, f32[9,64,256]{2,1,0:T(8,128)}, u32[]{:S(2)}, u32[]{:S(2)}) collective-permute-start(f32[9,64,256]{2,1,0:T(8,128)} %bitcast.241), channel_id=1, source_target_pairs={{0,3},{1,0},{2,1},{3,2},{4,7},{5,4},{6,5},{7,6},{8,11},{9,8},{10,9... | collective-permute-start | bytes 1769480 | tf_op jit(solution)/shard_map/ppermute | solution.py:95
  9.7 1.0 copy.27
  10.7 1.8 bitcast_convert_fusion
  12.5 8.7 %collective-permute-done.1 = f32[9,64,256]{2,1,0:T(8,128)} collective-permute-done((f32[9,64,256]{2,1,0:T(8,128)}, f32[9,64,256]{2,1,0:T(8,128)}, u32[]{:S(2)}, u32[]{:S(2)}) %collective-permute-start.1) | collective-permute-done | bytes 589856 | tf_op jit(solution)/shard_map/ppermute | solution.py:90
  21.2 2.5 %collective-permute-start.3 = (f32[9,64,256]{2,1,0:T(8,128)}, f32[9,64,256]{2,1,0:T(8,128)}, u32[]{:S(2)}, u32[]{:S(2)}) collective-permute-start(f32[9,64,256]{2,1,0:T(8,128)} %collective-permute-done.1), channel_id=1, source_target_pairs={{0,1},{1,2},{2,3},{3,0},{4,5},{5,6},{6,7},{7,4},{8,9},{9,10},{10,1... | collective-permute-start | bytes 1769480 | tf_op jit(solution)/shard_map/ppermute | solution.py:90
  23.8 119.3 %while.28 = (s32[]{:T(128)}, bf16[16,16,256]{2,1,0:T(8,128)(2,1)S(1)}, f32[9,256,256]{2,1,0:T(8,128)}, pred[]{:T(512)}, s32[]{:T(128)}, /*index=5*/bf16[2,16,16,...) while((s32[]{:T(128)}, ...), condition=%wide.region_3.4_spmd.clone, body=%wide.region_0.3_spmd.clone.sunk | while | flops 910100672 | bytes 44110644 | solution.py:75
  23.8 0.8 cosine_reduce_fusion.2
  27.0 1.4 fusion.102
  30.3 1.3 fusion.104
  31.6 1.6 scatter-add.71
  34.0 2.0 %add_select_fusion.2 = f32[16,16,256]{2,1,0:T(8,128)S(1)} fusion(f32[9,16,16,256]{3,2,1,0:T(8,128)S(1)} %convolution_bitcast_fusion.2, f32[18,18,256]{2,1,0:T(8,128)S(1)} %scatter-add.71, s32[]{:T(128)} %bitcast.237, s32[]{:T(128)} %bitcast.238, pred[]{:T(512)} %and_reduce_fusion.2), kind=kLoop, calls=%fused_computation.14.clone.1 | loop fusion | flops 131072 | bytes 786441 | tf_op jit(solution)/shard_map/select.85
  36.0 1.6 scatter-add.72
  39.3 1.1 fusion.112
  40.4 1.3 collective-permute-start
  41.8 3.4 %fusion.113 = f32[9,256,256]{2,1,0:T(8,128)} fusion(f32[9,256,256]{2,1,0:T(8,128)} %get-tuple-element.608, bf16[9,16,16,256]{3,2,0,1:T(8,128)(2,1)} %copy-done.8, pred[]{:T(512)S(6)} %compare.183, pred[]{:T(512)S(6)} %and.129, bf16[16,16,256]{2,1,0:T(8,128)(2,1)} %copy-done.6), kind=kOutput, calls=%fused_computation.2.clone.1 | convolution fusion | flops 304349184 | bytes 6029314 | tf_op jit(solution)/shard_map/while/body/eval_jaxpr/krcd,rce->kde/dot_general | solution.py:32
  45.2 2.1 %collective-permute-done = bf16[16,16,256]{2,1,0:T(8,128)(2,1)S(1)} collective-permute-done((bf16[16,16,256]{2,1,0:T(8,128)(2,1)S(1)}, bf16[16,16,256]{2,1,0:T(8,128)(2,1)S(1)}, u32[]{:S(2)}, u32[]{:S(2)}) %collective-permute-start) | collective-permute-done | bytes 131104 | tf_op jit(solution)/shard_map/while/body/eval_jaxpr/ppermute | solution.py:13
  47.3 0.8 cosine_reduce_fusion.2
  50.5 1.4 fusion.102
  53.9 1.3 fusion.104
  55.1 1.6 scatter-add.71
  57.5 2.0 %add_select_fusion.2 = f32[16,16,256]{2,1,0:T(8,128)S(1)} fusion(f32[9,16,16,256]{3,2,1,0:T(8,128)S(1)} %convolution_bitcast_fusion.2, f32[18,18,256]{2,1,0:T(8,128)S(1)} %scatter-add.71, s32[]{:T(128)} %bitcast.237, s32[]{:T(128)} %bitcast.238, pred[]{:T(512)} %and_reduce_fusion.2), kind=kLoop, calls=%fused_computation.14.clone.1 | loop fusion | flops 131072 | bytes 786441 | tf_op jit(solution)/shard_map/select.85
  59.5 1.6 scatter-add.72
  62.8 1.1 fusion.112
  63.9 1.3 collective-permute-start
  65.3 4.2 %fusion.113 = f32[9,256,256]{2,1,0:T(8,128)} fusion(f32[9,256,256]{2,1,0:T(8,128)} %get-tuple-element.608, bf16[9,16,16,256]{3,2,0,1:T(8,128)(2,1)} %copy-done.8, pred[]{:T(512)S(6)} %compare.183, pred[]{:T(512)S(6)} %and.129, bf16[16,16,256]{2,1,0:T(8,128)(2,1)} %copy-done.6), kind=kOutput, calls=%fused_computation.2.clone.1 | convolution fusion | flops 304349184 | bytes 6029314 | tf_op jit(solution)/shard_map/while/body/eval_jaxpr/krcd,rce->kde/dot_general | solution.py:32
  69.5 2.5 %collective-permute-done = bf16[16,16,256]{2,1,0:T(8,128)(2,1)S(1)} collective-permute-done((bf16[16,16,256]{2,1,0:T(8,128)(2,1)S(1)}, bf16[16,16,256]{2,1,0:T(8,128)(2,1)S(1)}, u32[]{:S(2)}, u32[]{:S(2)}) %collective-permute-start) | collective-permute-done | bytes 131104 | tf_op jit(solution)/shard_map/while/body/eval_jaxpr/ppermute | solution.py:13
  72.0 0.8 cosine_reduce_fusion.2
  75.2 1.4 fusion.102
  78.5 1.3 fusion.104
  79.8 1.6 scatter-add.71
  82.2 2.0 %add_select_fusion.2 = f32[16,16,256]{2,1,0:T(8,128)S(1)} fusion(f32[9,16,16,256]{3,2,1,0:T(8,128)S(1)} %convolution_bitcast_fusion.2, f32[18,18,256]{2,1,0:T(8,128)S(1)} %scatter-add.71, s32[]{:T(128)} %bitcast.237, s32[]{:T(128)} %bitcast.238, pred[]{:T(512)} %and_reduce_fusion.2), kind=kLoop, calls=%fused_computation.14.clone.1 | loop fusion | flops 131072 | bytes 786441 | tf_op jit(solution)/shard_map/select.85
  84.2 1.6 scatter-add.72
  87.5 1.1 fusion.112
  88.6 1.3 collective-permute-start
  89.9 4.2 %fusion.113 = f32[9,256,256]{2,1,0:T(8,128)} fusion(f32[9,256,256]{2,1,0:T(8,128)} %get-tuple-element.608, bf16[9,16,16,256]{3,2,0,1:T(8,128)(2,1)} %copy-done.8, pred[]{:T(512)S(6)} %compare.183, pred[]{:T(512)S(6)} %and.129, bf16[16,16,256]{2,1,0:T(8,128)(2,1)} %copy-done.6), kind=kOutput, calls=%fused_computation.2.clone.1 | convolution fusion | flops 304349184 | bytes 6029314 | tf_op jit(solution)/shard_map/while/body/eval_jaxpr/krcd,rce->kde/dot_general | solution.py:32
  94.1 1.9 collective-permute-done
  96.0 0.8 cosine_reduce_fusion.2
  99.2 1.4 fusion.102
  102.6 1.3 fusion.104
  103.9 1.6 scatter-add.71
  106.2 2.0 %add_select_fusion.2 = f32[16,16,256]{2,1,0:T(8,128)S(1)} fusion(f32[9,16,16,256]{3,2,1,0:T(8,128)S(1)} %convolution_bitcast_fusion.2, f32[18,18,256]{2,1,0:T(8,128)S(1)} %scatter-add.71, s32[]{:T(128)} %bitcast.237, s32[]{:T(128)} %bitcast.238, pred[]{:T(512)} %and_reduce_fusion.2), kind=kLoop, calls=%fused_computation.14.clone.1 | loop fusion | flops 131072 | bytes 786441 | tf_op jit(solution)/shard_map/select.85
  108.2 1.6 scatter-add.72
  111.6 1.1 fusion.112
  112.7 1.3 collective-permute-start
  114.0 4.2 %fusion.113 = f32[9,256,256]{2,1,0:T(8,128)} fusion(f32[9,256,256]{2,1,0:T(8,128)} %get-tuple-element.608, bf16[9,16,16,256]{3,2,0,1:T(8,128)(2,1)} %copy-done.8, pred[]{:T(512)S(6)} %compare.183, pred[]{:T(512)S(6)} %and.129, bf16[16,16,256]{2,1,0:T(8,128)(2,1)} %copy-done.6), kind=kOutput, calls=%fused_computation.2.clone.1 | convolution fusion | flops 304349184 | bytes 6029314 | tf_op jit(solution)/shard_map/while/body/eval_jaxpr/krcd,rce->kde/dot_general | solution.py:32
  118.2 1.3 collective-permute-done
  122.8 1.4 fusion.102
  126.1 1.3 fusion.104
  127.4 1.6 scatter-add.71
  129.7 2.0 %add_select_fusion.2 = f32[16,16,256]{2,1,0:T(8,128)S(1)} fusion(f32[9,16,16,256]{3,2,1,0:T(8,128)S(1)} %convolution_bitcast_fusion.2, f32[18,18,256]{2,1,0:T(8,128)S(1)} %scatter-add.71, s32[]{:T(128)} %bitcast.237, s32[]{:T(128)} %bitcast.238, pred[]{:T(512)} %and_reduce_fusion.2), kind=kLoop, calls=%fused_computation.14.clone.1 | loop fusion | flops 131072 | bytes 786441 | tf_op jit(solution)/shard_map/select.85
  131.7 1.6 scatter-add.72
  135.1 1.1 fusion.112
  136.2 1.3 collective-permute-start
  137.5 4.2 %fusion.113 = f32[9,256,256]{2,1,0:T(8,128)} fusion(f32[9,256,256]{2,1,0:T(8,128)} %get-tuple-element.608, bf16[9,16,16,256]{3,2,0,1:T(8,128)(2,1)} %copy-done.8, pred[]{:T(512)S(6)} %compare.183, pred[]{:T(512)S(6)} %and.129, bf16[16,16,256]{2,1,0:T(8,128)(2,1)} %copy-done.6), kind=kOutput, calls=%fused_computation.2.clone.1 | convolution fusion | flops 304349184 | bytes 6029314 | tf_op jit(solution)/shard_map/while/body/eval_jaxpr/krcd,rce->kde/dot_general | solution.py:32
  141.7 1.3 collective-permute-done
  143.0 3.3 %fusion.56 = bf16[9,256,256]{2,1,0:T(8,128)(2,1)} fusion(f32[9,256,256]{2,1,0:T(8,128)} %get-tuple-element.472, bf16[1,1,9,256,256]{4,3,2,1,0:T(8,128)(2,1)} %param.29), kind=kLoop, calls=%fused_computation.72 | loop fusion | flops 2359296 | bytes 4718592 | tf_op jit(solution)/shard_map/convert_element_type | solution.py:76
  146.4 1.6 broadcast.430
  148.0 0.9 constant_dynamic-update-slice_fusion.3
  148.9 2.0 %constant_dynamic-update-slice_fusion.2 = f32[9,256,256]{2,1,0:T(8,128)} fusion(f32[9,256,256]{2,1,0:T(8,128)} %constant_dynamic-update-slice_fusion.3, f32[9,64,256]{2,1,0:T(8,128)} %collective-permute-done.1, s32[]{:T(128)S(6)} %select_n.85), kind=kLoop, calls=%fused_computation.82 | loop fusion | bytes 1179652 | tf_op jit(solution)/shard_map/dynamic_update_slice | solution.py:91
  150.9 1.9 constant_dynamic-update-slice_fusion.1
  152.8 1.9 constant_dynamic-update-slice_fusion
  154.8 28.5 %all-reduce.4.cloned.1.call-done = bf16[9,256,256]{2,1,0:T(8,128)(2,1)} async-done(((bf16[9,256,256]{2,1,0:T(8,128)(2,1)}), bf16[9,256,256]{2,1,0:T(8,128)(2,1)}) %all-reduce.4.cloned.1.call-update) | async-done | bytes 1179664 | tf_op jit(solution)/shard_map/psum | solution.py:82
  183.3 4.0 %multiply_add_fusion = (f32[9,256,256]{2,1,0:T(8,128)S(1)}, f32[1,9,256,256]{3,2,1,0:T(8,128)}) fusion(f32[9,256,256]{2,1,0:T(8,128)} %constant_dynamic-update-slice_fusion, bf16[9,256,256]{2,1,0:T(8,128)(2,1)} %all-reduce.4.cloned.1.call-done, f32[1,9,256,256]{3,2,1,0:T(8,128)S(1)} %copy-done.4), kind=kLoop, calls=%fused_computation.76 | loop fusion | flops 4718592 | bytes 10616832 | tf_op jit(solution)/shard_map/add | solution.py:101
  187.3 0.9 dynamic-slice_bitcast_fusion.1
  (236 shorter events, 28.1 us)
Async XLA Ops:
  7.2 16.6 %copy-start.9 = (s32[3]{0:T(128)S(1)}, s32[3]{0:T(128)}, u32[]{:S(2)}) copy-start(s32[3]{0:T(128)} %constant.622.clone.2) | copy-start | bytes 40
  7.2 16.6 %copy-start.10 = (s32[1,2]{1,0:T(1,128)S(1)}, s32[1,2]{1,0:T(1,128)}, u32[]{:S(2)}) copy-start(s32[1,2]{1,0:T(1,128)} %param.28) | copy-start | bytes 28
  7.2 176.1 %all-reduce.4.cloned.1.call-start = ((), (), s32[]{:S(2)}) async-start(), calls=%async_computation | async-start | bytes 2359296 | tf_op jit(solution)/shard_map/psum | solution.py:82
  7.2 14.0 %collective-permute-start.1 = (f32[9,64,256]{2,1,0:T(8,128)}, f32[9,64,256]{2,1,0:T(8,128)}, u32[]{:S(2)}, u32[]{:S(2)}) collective-permute-start(f32[9,64,256]{2,1,0:T(8,128)} %bitcast.240), channel_id=1, source_target_pairs={{0,1},{1,2},{2,3},{3,0},{4,5},{5,6},{6,7},{7,4},{8,9},{9,10},{10,1... | collective-permute-start | bytes 1769480 | tf_op jit(solution)/shard_map/ppermute | solution.py:90
  7.7 143.2 %collective-permute-start.2 = (f32[9,64,256]{2,1,0:T(8,128)}, f32[9,64,256]{2,1,0:T(8,128)}, u32[]{:S(2)}, u32[]{:S(2)}) collective-permute-start(f32[9,64,256]{2,1,0:T(8,128)} %bitcast.241), channel_id=1, source_target_pairs={{0,3},{1,0},{2,1},{3,2},{4,7},{5,4},{6,5},{7,6},{8,11},{9,8},{10,9... | collective-permute-start | bytes 1769480 | tf_op jit(solution)/shard_map/ppermute | solution.py:95
  21.2 131.6 %collective-permute-start.3 = (f32[9,64,256]{2,1,0:T(8,128)}, f32[9,64,256]{2,1,0:T(8,128)}, u32[]{:S(2)}, u32[]{:S(2)}) collective-permute-start(f32[9,64,256]{2,1,0:T(8,128)} %collective-permute-done.1), channel_id=1, source_target_pairs={{0,1},{1,2},{2,3},{3,0},{4,5},{5,6},{6,7},{7,4},{8,9},{9,10},{10,1... | collective-permute-start | bytes 1769480 | tf_op jit(solution)/shard_map/ppermute | solution.py:90
  23.8 3.2 %copy-start.2 = (bf16[2,16,16,256]{3,2,0,1:T(8,128)(2,1)}, bf16[2,16,16,256]{3,2,0,1:T(8,128)(2,1)S(1)}, u32[]{:S(2)}) copy-start(bf16[2,16,16,256]{3,2,0,1:T(8,128)(2,1)S(1)} %get-tuple-element.629) | copy-start | bytes 786436 | tf_op jit(solution)/shard_map/while
  23.8 3.2 %copy-start.5 = (bf16[16,16,256]{2,1,0:T(8,128)(2,1)}, bf16[16,16,256]{2,1,0:T(8,128)(2,1)S(1)}, u32[]{:S(2)}) copy-start(bf16[16,16,256]{2,1,0:T(8,128)(2,1)S(1)} %get-tuple-element.607) | copy-start | bytes 393220 | tf_op jit(solution)/shard_map/while
  23.8 4.6 %copy-start = (bf16[9,256,256]{2,1,0:T(8,128)(2,1)}, bf16[9,256,256]{2,1,0:T(8,128)(2,1)S(1)}, u32[]{:S(2)}) copy-start(bf16[9,256,256]{2,1,0:T(8,128)(2,1)S(1)} %get-tuple-element.630) | copy-start | bytes 3538948 | tf_op jit(solution)/shard_map/while
  24.9 2.1 %copy-start.8 = (bf16[9,16,16,256]{3,2,0,1:T(8,128)(2,1)}, bf16[9,16,16,256]{3,2,0,1:T(8,128)(2,1)S(1)}, u32[]{:S(2)}) copy-start(bf16[9,16,16,256]{3,2,0,1:T(8,128)(2,1)S(1)} %fusion.101) | copy-start | bytes 3538948 | tf_op jit(solution)/shard_map/while
  28.4 1.9 copy-start.6
  40.4 6.9 %collective-permute-start = (bf16[16,16,256]{2,1,0:T(8,128)(2,1)S(1)}, bf16[16,16,256]{2,1,0:T(8,128)(2,1)S(1)}, u32[]{:S(2)}, u32[]{:S(2)}) collective-permute-start(bf16[16,16,256]{2,1,0:T(8,128)(2,1)S(1)} %fusion.112), channel_id=1, source_target_pairs={{4,0},{8,4},{12,8},{5,1},{9,5},{13,9},{6,2},{10,6},{14,10},{7,3},{... | collective-permute-start | bytes 393224 | tf_op jit(solution)/shard_map/while/body/eval_jaxpr/ppermute | solution.py:13
  41.7 5.6 %copy-start.1 = (bf16[9,256,256]{2,1,0:T(8,128)(2,1)S(1)}, bf16[9,256,256]{2,1,0:T(8,128)(2,1)}, u32[]{:S(2)}) copy-start(bf16[9,256,256]{2,1,0:T(8,128)(2,1)} %copy-done) | copy-start | bytes 3538948 | tf_op jit(solution)/shard_map/while
  41.8 5.5 %copy-start.3 = (bf16[2,16,16,256]{3,2,0,1:T(8,128)(2,1)S(1)}, bf16[2,16,16,256]{3,2,0,1:T(8,128)(2,1)}, u32[]{:S(2)}) copy-start(bf16[2,16,16,256]{3,2,0,1:T(8,128)(2,1)} %copy-done.2) | copy-start | bytes 786436 | tf_op jit(solution)/shard_map/while
  47.3 3.2 %copy-start.2 = (bf16[2,16,16,256]{3,2,0,1:T(8,128)(2,1)}, bf16[2,16,16,256]{3,2,0,1:T(8,128)(2,1)S(1)}, u32[]{:S(2)}) copy-start(bf16[2,16,16,256]{3,2,0,1:T(8,128)(2,1)S(1)} %get-tuple-element.629) | copy-start | bytes 786436 | tf_op jit(solution)/shard_map/while
  47.3 3.2 %copy-start.5 = (bf16[16,16,256]{2,1,0:T(8,128)(2,1)}, bf16[16,16,256]{2,1,0:T(8,128)(2,1)S(1)}, u32[]{:S(2)}) copy-start(bf16[16,16,256]{2,1,0:T(8,128)(2,1)S(1)} %get-tuple-element.607) | copy-start | bytes 393220 | tf_op jit(solution)/shard_map/while
  47.3 4.6 %copy-start = (bf16[9,256,256]{2,1,0:T(8,128)(2,1)}, bf16[9,256,256]{2,1,0:T(8,128)(2,1)S(1)}, u32[]{:S(2)}) copy-start(bf16[9,256,256]{2,1,0:T(8,128)(2,1)S(1)} %get-tuple-element.630) | copy-start | bytes 3538948 | tf_op jit(solution)/shard_map/while
  48.4 2.1 %copy-start.8 = (bf16[9,16,16,256]{3,2,0,1:T(8,128)(2,1)}, bf16[9,16,16,256]{3,2,0,1:T(8,128)(2,1)S(1)}, u32[]{:S(2)}) copy-start(bf16[9,16,16,256]{3,2,0,1:T(8,128)(2,1)S(1)} %fusion.101) | copy-start | bytes 3538948 | tf_op jit(solution)/shard_map/while
  52.0 1.9 copy-start.6
  63.9 8.0 %collective-permute-start = (bf16[16,16,256]{2,1,0:T(8,128)(2,1)S(1)}, bf16[16,16,256]{2,1,0:T(8,128)(2,1)S(1)}, u32[]{:S(2)}, u32[]{:S(2)}) collective-permute-start(bf16[16,16,256]{2,1,0:T(8,128)(2,1)S(1)} %fusion.112), channel_id=1, source_target_pairs={{4,0},{8,4},{12,8},{5,1},{9,5},{13,9},{6,2},{10,6},{14,10},{7,3},{... | collective-permute-start | bytes 393224 | tf_op jit(solution)/shard_map/while/body/eval_jaxpr/ppermute | solution.py:13
  65.3 6.7 %copy-start.1 = (bf16[9,256,256]{2,1,0:T(8,128)(2,1)S(1)}, bf16[9,256,256]{2,1,0:T(8,128)(2,1)}, u32[]{:S(2)}) copy-start(bf16[9,256,256]{2,1,0:T(8,128)(2,1)} %copy-done) | copy-start | bytes 3538948 | tf_op jit(solution)/shard_map/while
  65.3 6.7 %copy-start.3 = (bf16[2,16,16,256]{3,2,0,1:T(8,128)(2,1)S(1)}, bf16[2,16,16,256]{3,2,0,1:T(8,128)(2,1)}, u32[]{:S(2)}) copy-start(bf16[2,16,16,256]{3,2,0,1:T(8,128)(2,1)} %copy-done.2) | copy-start | bytes 786436 | tf_op jit(solution)/shard_map/while
  72.0 3.2 %copy-start.2 = (bf16[2,16,16,256]{3,2,0,1:T(8,128)(2,1)}, bf16[2,16,16,256]{3,2,0,1:T(8,128)(2,1)S(1)}, u32[]{:S(2)}) copy-start(bf16[2,16,16,256]{3,2,0,1:T(8,128)(2,1)S(1)} %get-tuple-element.629) | copy-start | bytes 786436 | tf_op jit(solution)/shard_map/while
  72.0 3.2 %copy-start.5 = (bf16[16,16,256]{2,1,0:T(8,128)(2,1)}, bf16[16,16,256]{2,1,0:T(8,128)(2,1)S(1)}, u32[]{:S(2)}) copy-start(bf16[16,16,256]{2,1,0:T(8,128)(2,1)S(1)} %get-tuple-element.607) | copy-start | bytes 393220 | tf_op jit(solution)/shard_map/while
  72.0 4.6 %copy-start = (bf16[9,256,256]{2,1,0:T(8,128)(2,1)}, bf16[9,256,256]{2,1,0:T(8,128)(2,1)S(1)}, u32[]{:S(2)}) copy-start(bf16[9,256,256]{2,1,0:T(8,128)(2,1)S(1)} %get-tuple-element.630) | copy-start | bytes 3538948 | tf_op jit(solution)/shard_map/while
  73.1 2.1 %copy-start.8 = (bf16[9,16,16,256]{3,2,0,1:T(8,128)(2,1)}, bf16[9,16,16,256]{3,2,0,1:T(8,128)(2,1)S(1)}, u32[]{:S(2)}) copy-start(bf16[9,16,16,256]{3,2,0,1:T(8,128)(2,1)S(1)} %fusion.101) | copy-start | bytes 3538948 | tf_op jit(solution)/shard_map/while
  76.6 1.9 copy-start.6
  88.6 7.4 %collective-permute-start = (bf16[16,16,256]{2,1,0:T(8,128)(2,1)S(1)}, bf16[16,16,256]{2,1,0:T(8,128)(2,1)S(1)}, u32[]{:S(2)}, u32[]{:S(2)}) collective-permute-start(bf16[16,16,256]{2,1,0:T(8,128)(2,1)S(1)} %fusion.112), channel_id=1, source_target_pairs={{4,0},{8,4},{12,8},{5,1},{9,5},{13,9},{6,2},{10,6},{14,10},{7,3},{... | collective-permute-start | bytes 393224 | tf_op jit(solution)/shard_map/while/body/eval_jaxpr/ppermute | solution.py:13
  89.9 6.1 %copy-start.1 = (bf16[9,256,256]{2,1,0:T(8,128)(2,1)S(1)}, bf16[9,256,256]{2,1,0:T(8,128)(2,1)}, u32[]{:S(2)}) copy-start(bf16[9,256,256]{2,1,0:T(8,128)(2,1)} %copy-done) | copy-start | bytes 3538948 | tf_op jit(solution)/shard_map/while
  89.9 6.1 %copy-start.3 = (bf16[2,16,16,256]{3,2,0,1:T(8,128)(2,1)S(1)}, bf16[2,16,16,256]{3,2,0,1:T(8,128)(2,1)}, u32[]{:S(2)}) copy-start(bf16[2,16,16,256]{3,2,0,1:T(8,128)(2,1)} %copy-done.2) | copy-start | bytes 786436 | tf_op jit(solution)/shard_map/while
  96.0 3.2 %copy-start.2 = (bf16[2,16,16,256]{3,2,0,1:T(8,128)(2,1)}, bf16[2,16,16,256]{3,2,0,1:T(8,128)(2,1)S(1)}, u32[]{:S(2)}) copy-start(bf16[2,16,16,256]{3,2,0,1:T(8,128)(2,1)S(1)} %get-tuple-element.629) | copy-start | bytes 786436 | tf_op jit(solution)/shard_map/while
  96.0 3.2 %copy-start.5 = (bf16[16,16,256]{2,1,0:T(8,128)(2,1)}, bf16[16,16,256]{2,1,0:T(8,128)(2,1)S(1)}, u32[]{:S(2)}) copy-start(bf16[16,16,256]{2,1,0:T(8,128)(2,1)S(1)} %get-tuple-element.607) | copy-start | bytes 393220 | tf_op jit(solution)/shard_map/while
  96.0 4.6 %copy-start = (bf16[9,256,256]{2,1,0:T(8,128)(2,1)}, bf16[9,256,256]{2,1,0:T(8,128)(2,1)S(1)}, u32[]{:S(2)}) copy-start(bf16[9,256,256]{2,1,0:T(8,128)(2,1)S(1)} %get-tuple-element.630) | copy-start | bytes 3538948 | tf_op jit(solution)/shard_map/while
  97.2 2.1 %copy-start.8 = (bf16[9,16,16,256]{3,2,0,1:T(8,128)(2,1)}, bf16[9,16,16,256]{3,2,0,1:T(8,128)(2,1)S(1)}, u32[]{:S(2)}) copy-start(bf16[9,16,16,256]{3,2,0,1:T(8,128)(2,1)S(1)} %fusion.101) | copy-start | bytes 3538948 | tf_op jit(solution)/shard_map/while
  100.7 1.9 copy-start.6
  112.7 6.9 %collective-permute-start = (bf16[16,16,256]{2,1,0:T(8,128)(2,1)S(1)}, bf16[16,16,256]{2,1,0:T(8,128)(2,1)S(1)}, u32[]{:S(2)}, u32[]{:S(2)}) collective-permute-start(bf16[16,16,256]{2,1,0:T(8,128)(2,1)S(1)} %fusion.112), channel_id=1, source_target_pairs={{4,0},{8,4},{12,8},{5,1},{9,5},{13,9},{6,2},{10,6},{14,10},{7,3},{... | collective-permute-start | bytes 393224 | tf_op jit(solution)/shard_map/while/body/eval_jaxpr/ppermute | solution.py:13
  114.0 5.6 %copy-start.1 = (bf16[9,256,256]{2,1,0:T(8,128)(2,1)S(1)}, bf16[9,256,256]{2,1,0:T(8,128)(2,1)}, u32[]{:S(2)}) copy-start(bf16[9,256,256]{2,1,0:T(8,128)(2,1)} %copy-done) | copy-start | bytes 3538948 | tf_op jit(solution)/shard_map/while
  114.0 5.5 %copy-start.3 = (bf16[2,16,16,256]{3,2,0,1:T(8,128)(2,1)S(1)}, bf16[2,16,16,256]{3,2,0,1:T(8,128)(2,1)}, u32[]{:S(2)}) copy-start(bf16[2,16,16,256]{3,2,0,1:T(8,128)(2,1)} %copy-done.2) | copy-start | bytes 786436 | tf_op jit(solution)/shard_map/while
  119.5 3.2 %copy-start.2 = (bf16[2,16,16,256]{3,2,0,1:T(8,128)(2,1)}, bf16[2,16,16,256]{3,2,0,1:T(8,128)(2,1)S(1)}, u32[]{:S(2)}) copy-start(bf16[2,16,16,256]{3,2,0,1:T(8,128)(2,1)S(1)} %get-tuple-element.629) | copy-start | bytes 786436 | tf_op jit(solution)/shard_map/while
  119.5 3.2 %copy-start.5 = (bf16[16,16,256]{2,1,0:T(8,128)(2,1)}, bf16[16,16,256]{2,1,0:T(8,128)(2,1)S(1)}, u32[]{:S(2)}) copy-start(bf16[16,16,256]{2,1,0:T(8,128)(2,1)S(1)} %get-tuple-element.607) | copy-start | bytes 393220 | tf_op jit(solution)/shard_map/while
  119.5 4.6 %copy-start = (bf16[9,256,256]{2,1,0:T(8,128)(2,1)}, bf16[9,256,256]{2,1,0:T(8,128)(2,1)S(1)}, u32[]{:S(2)}) copy-start(bf16[9,256,256]{2,1,0:T(8,128)(2,1)S(1)} %get-tuple-element.630) | copy-start | bytes 3538948 | tf_op jit(solution)/shard_map/while
  120.7 2.1 %copy-start.8 = (bf16[9,16,16,256]{3,2,0,1:T(8,128)(2,1)}, bf16[9,16,16,256]{3,2,0,1:T(8,128)(2,1)S(1)}, u32[]{:S(2)}) copy-start(bf16[9,16,16,256]{3,2,0,1:T(8,128)(2,1)S(1)} %fusion.101) | copy-start | bytes 3538948 | tf_op jit(solution)/shard_map/while
  124.2 1.9 copy-start.6
  136.2 6.9 %collective-permute-start = (bf16[16,16,256]{2,1,0:T(8,128)(2,1)S(1)}, bf16[16,16,256]{2,1,0:T(8,128)(2,1)S(1)}, u32[]{:S(2)}, u32[]{:S(2)}) collective-permute-start(bf16[16,16,256]{2,1,0:T(8,128)(2,1)S(1)} %fusion.112), channel_id=1, source_target_pairs={{4,0},{8,4},{12,8},{5,1},{9,5},{13,9},{6,2},{10,6},{14,10},{7,3},{... | collective-permute-start | bytes 393224 | tf_op jit(solution)/shard_map/while/body/eval_jaxpr/ppermute | solution.py:13
  137.5 5.6 %copy-start.1 = (bf16[9,256,256]{2,1,0:T(8,128)(2,1)S(1)}, bf16[9,256,256]{2,1,0:T(8,128)(2,1)}, u32[]{:S(2)}) copy-start(bf16[9,256,256]{2,1,0:T(8,128)(2,1)} %copy-done) | copy-start | bytes 3538948 | tf_op jit(solution)/shard_map/while
  137.5 5.5 %copy-start.3 = (bf16[2,16,16,256]{3,2,0,1:T(8,128)(2,1)S(1)}, bf16[2,16,16,256]{3,2,0,1:T(8,128)(2,1)}, u32[]{:S(2)}) copy-start(bf16[2,16,16,256]{3,2,0,1:T(8,128)(2,1)} %copy-done.2) | copy-start | bytes 786436 | tf_op jit(solution)/shard_map/while
  146.3 1.7 copy-start.7
  148.0 35.2 %copy-start.4 = (f32[1,9,256,256]{3,2,1,0:T(8,128)S(1)}, f32[1,9,256,256]{3,2,1,0:T(8,128)}, u32[]{:S(2)}) copy-start(f32[1,9,256,256]{3,2,1,0:T(8,128)} %param.30) | copy-start | bytes 7077892
Sparse Core Ops, SparseCore 0:
  146.5 36.7 all-reduce.3
